TPU v7x, 256 devices: a whole 4x4x8 slice. The times are simulated.
256 devices in a mesh: dp: 16 (over x, y), seq: 16 (over z, core).
Axes of the slice: x: 4, y: 4, z: 8, core: 2. Of those that a mesh axis runs over, the one named last changes fastest.
Arguments:
- tokens: bfloat16 [49152, 4096], P(('dp', 'seq')), parts along dimension 0, may hold values from -72 to 72
- monarch_inner_factor: bfloat16 [3, 64, 64, 64], replicated, may hold values from -0.75 to 0.75
- monarch_outer_factor: bfloat16 [3, 64, 64, 64], replicated, may hold values from -0.75 to 0.75
- adapter_down_weight: bfloat16 [3, 4096, 16], replicated, may hold values from -0.09375 to 0.09375
- adapter_up_weight: bfloat16 [3, 16, 4096], replicated, may hold values from -1.5 to 1.5
- pattern: int32 [768, 3], P('dp'), parts along dimension 0, may hold values from 2 to 47, as said below
Outputs:
- context: bfloat16 [49152, 4096], P(('dp', 'seq')), parts along dimension 0
There are 16 independent parts, one for each index of `dp`. A program takes and returns all parts, laid end to end along the dimension named above; an argument that names none is the same for every part. Nothing has to cross between parts.
Inputs may be any that keep to these rules, and one draw needn't show every extreme that they name: `pattern`: row b names the random key blocks of query block b. The 9 entries of the rows of one index of seq name at most 1 block held by any one index of seq, and exactly 1 of some index's blocks. A block may be named more than once.
All inputs are finite; a program needn't handle non-finite values.
Results may differ from a plain program's by a relative error of at most 0.012.
The roundings to bfloat16 on the way count: a program that leaves them out, or rounds other values in their place, can miss the bound.
Values may be sent and summed in bfloat16 or wider, within the bound.
No kernel may reach another device: no remote copies, remote signals or barrier semaphores. Data moves between devices by JAX's collectives and lax.ppermute only.
A program may use at most 192 MiB of HBM per device.

v0:
```python
import jax
import jax.numpy as jnp
from jax import lax
from jax.sharding import PartitionSpec as P

HEADS = 32
HD = 128
BLK = 64
RAND = 3
GLOB_BLOCKS = 2


def spread(value, axis, root):
    mine = lax.axis_index(axis) == root
    return lax.psum(jnp.where(mine, value, jnp.zeros_like(value)), axis)


def padded_2(value, sides, width):
    for axis, dim in sides:
        size, length = (lax.axis_size(axis), value.shape[dim])
        up = [(i, (i + 1) % size) for i in range(size - 1)]
        down = [(j, i) for i, j in up]
        last = lax.slice_in_dim(value, length - width, length, axis=dim)
        initial = lax.slice_in_dim(value, 0, width, axis=dim)
        before = lax.ppermute(last, axis, up)
        after = lax.ppermute(initial, axis, down)
        value = jnp.concatenate([before, value, after], axis=dim)
    return value


def combined_all(value, axis, join):
    pieces = jax.tree.map(lambda part: lax.all_gather(part, axis), value)
    head = jax.tree.map(lambda part: part[0], pieces)
    tail = jax.tree.map(lambda part: part[1:], pieces)
    so_far, _ = lax.scan(lambda so_far, piece: (join(so_far, piece), None), head, tail)
    return so_far


def apply_projection(
    tokens, monarch_inner_factor, monarch_outer_factor, adapter_down_weight, adapter_up_weight
):
    row_count, feature_count = tokens.shape
    proj_count = monarch_inner_factor.shape[0]
    block_count = monarch_inner_factor.shape[1]
    split_rows = tokens.reshape(row_count, block_count, block_count)
    inner_rows = jnp.einsum(
        "tai,paij->ptaj", split_rows, monarch_inner_factor, preferred_element_type=jnp.float32
    ).astype(jnp.bfloat16)
    main_part = jnp.einsum(
        "ptaj,pjak->ptjk", inner_rows, monarch_outer_factor, preferred_element_type=jnp.float32
    )
    adapter_update = jnp.einsum(
        "kg,vgj->vkj", tokens, adapter_down_weight, preferred_element_type=jnp.float32
    ).astype(jnp.bfloat16)
    adapter_lifted_rows = jnp.einsum(
        "bcj,bjf->bcf", adapter_update, adapter_up_weight, preferred_element_type=jnp.float32
    )
    return (main_part.reshape(proj_count, row_count, feature_count) + adapter_lifted_rows).astype(
        jnp.bfloat16
    )


def to_heads(rows):
    proj_count, row_count, feature_count = rows.shape
    return jnp.transpose(
        rows.reshape(proj_count, row_count, HEADS, feature_count // HEADS), (0, 2, 1, 3)
    )


def combine(part_one, part_two):
    peak_one, total_one, numer_one = part_one
    peak_two, total_two, numer_two = part_two
    joint_peak = jnp.maximum(peak_one, peak_two)
    factor_one = jnp.exp(peak_one - joint_peak)
    factor_two = jnp.exp(peak_two - joint_peak)
    joint_total = total_one * factor_one + total_two * factor_two
    joint_numer = numer_one * factor_one[:, :, None] + numer_two * factor_two[:, :, None]
    return (joint_peak, joint_total, joint_numer)


def per_device(
    tokens,
    monarch_inner_factor,
    monarch_outer_factor,
    adapter_down_weight,
    adapter_up_weight,
    pattern,
):
    tok_rows, feature_count = tokens.shape
    head_size = feature_count // HEADS
    local_blocks = tok_rows // BLK
    seq_count = lax.axis_size("seq")
    seq_index = lax.axis_index("seq")
    block_total = seq_count * local_blocks
    global_rows = GLOB_BLOCKS * BLK
    request_count = local_blocks * RAND
    slot_count = (request_count + seq_count - 1) // seq_count
    score_scale = float(HD) ** (-0.5)
    projected_rows = apply_projection(
        tokens, monarch_inner_factor, monarch_outer_factor, adapter_down_weight, adapter_up_weight
    )
    head_rows_all = to_heads(projected_rows)
    key_value = head_rows_all[1:]
    picked = pattern.reshape(seq_count, request_count)
    source_dev = picked // local_blocks
    within = picked % local_blocks
    req_order = jnp.arange(request_count, dtype=jnp.int32)
    same_source = source_dev[:, :, None] == source_dev[:, None, :]
    earlier = req_order[None, :] < req_order[:, None]
    slot_rank = jnp.sum((same_source & earlier[None]).astype(jnp.int32), axis=2)
    slot_ids = jnp.arange(slot_count, dtype=jnp.int32)
    matches = (source_dev == seq_index)[:, None, :] & (
        slot_rank[:, None, :] == slot_ids[None, :, None]
    )
    present = jnp.any(matches, axis=2)
    chosen = jnp.sum(jnp.where(matches, within[:, None, :], 0), axis=2)
    my_source = lax.dynamic_index_in_dim(source_dev, seq_index, 0, keepdims=False)
    my_rank = lax.dynamic_index_in_dim(slot_rank, seq_index, 0, keepdims=False)
    fetch_index = my_source * slot_count + my_rank
    zero_value = jnp.zeros((), jnp.bfloat16)
    global_heads = spread(head_rows_all[:, :, :global_rows], "seq", 0)
    padded = padded_2(key_value, (("seq", 2),), BLK)
    kv_blocks = key_value.reshape(2, HEADS, local_blocks, BLK, head_size)
    outgoing = jnp.take(kv_blocks, chosen.reshape(-1), axis=2).reshape(
        2, HEADS, seq_count, slot_count, BLK, head_size
    )
    outgoing = jnp.where(present[None, None, :, :, None, None], outgoing, zero_value)
    incoming = lax.all_to_all(outgoing, "seq", split_axis=2, concat_axis=2, tiled=True)
    random_kv = jnp.take(
        incoming.reshape(2, HEADS, seq_count * slot_count, BLK, head_size), fetch_index, axis=2
    )
    random_keys = random_kv.reshape(2, HEADS, local_blocks, RAND * BLK, head_size)
    padded_blocks = padded.reshape(2, HEADS, local_blocks + 2, BLK, head_size)
    local_kv = jnp.concatenate(
        [
            padded_blocks[:, :, 0:local_blocks],
            padded_blocks[:, :, 1 : local_blocks + 1],
            padded_blocks[:, :, 2 : local_blocks + 2],
            random_keys,
        ],
        axis=3,
    )
    block_ids = seq_index * local_blocks + jnp.arange(local_blocks, dtype=jnp.int32)
    window_blocks = block_ids[:, None] + jnp.arange(-1, 2, dtype=jnp.int32)[None, :]
    window_valid = (window_blocks >= GLOB_BLOCKS) & (window_blocks < block_total)
    always_random = jnp.zeros((local_blocks, RAND * BLK), jnp.int32) == 0
    key_valid = jnp.concatenate([jnp.repeat(window_valid, BLK, axis=1), always_random], axis=1)
    query_blocks = head_rows_all[0].reshape(HEADS, local_blocks, BLK, head_size)
    global_keys = global_heads[1]
    global_values = global_heads[2]
    local_scores = (
        jnp.einsum("hbqe,hbke->hbqk", query_blocks, local_kv[0], preferred_element_type=jnp.float32)
        * score_scale
    )
    local_scores = jnp.where(key_valid[None, :, None, :], local_scores, -jnp.inf)
    glob_scores = (
        jnp.einsum("hbqe,hge->hbqg", query_blocks, global_keys, preferred_element_type=jnp.float32)
        * score_scale
    )
    row_peak = jnp.maximum(jnp.max(local_scores, axis=-1), jnp.max(glob_scores, axis=-1))
    local_weights = jnp.exp(local_scores - row_peak[..., None])
    glob_weights = jnp.exp(glob_scores - row_peak[..., None])
    row_total = jnp.sum(local_weights, axis=-1) + jnp.sum(glob_weights, axis=-1)
    local_numer = jnp.einsum(
        "hbqk,hbke->hbqe",
        local_weights.astype(jnp.bfloat16),
        local_kv[1],
        preferred_element_type=jnp.float32,
    )
    glob_numer = jnp.einsum(
        "hbqg,hge->hbqe",
        glob_weights.astype(jnp.bfloat16),
        global_values,
        preferred_element_type=jnp.float32,
    )
    mixed = (local_numer + glob_numer) / row_total[..., None]
    local_out = (
        jnp.transpose(mixed.reshape(HEADS, tok_rows, head_size), (1, 0, 2))
        .reshape(tok_rows, feature_count)
        .astype(jnp.bfloat16)
    )
    global_query = global_heads[0]
    global_scores = (
        jnp.einsum(
            "hqe,hke->hqk", global_query, head_rows_all[1], preferred_element_type=jnp.float32
        )
        * score_scale
    )
    global_peak = jnp.max(global_scores, axis=-1)
    global_weights = jnp.exp(global_scores - global_peak[:, :, None])
    global_total = jnp.sum(global_weights, axis=-1)
    global_numer = jnp.einsum(
        "hqk,hke->hqe",
        global_weights.astype(jnp.bfloat16),
        head_rows_all[2],
        preferred_element_type=jnp.float32,
    )
    merged = combined_all((global_peak, global_total, global_numer), "seq", combine)
    head_mixed = merged[2] / merged[1][:, :, None]
    head_out = (
        jnp.transpose(head_mixed, (1, 0, 2))
        .reshape(global_rows, feature_count)
        .astype(jnp.bfloat16)
    )
    head_rows = jnp.where(seq_index == 0, head_out, local_out[:global_rows])
    return jnp.concatenate([head_rows, local_out[global_rows:]], axis=0)


def solution(mesh):
    return jax.shard_map(
        per_device,
        mesh=mesh,
        in_specs=(P(("dp", "seq"), None), P(), P(), P(), P(), P("dp", None)),
        out_specs=P(("dp", "seq"), None),
        check_vma=False,
    )
```

profile of v0, /device:TPU:1, one launch (start us, length us, event | category | flops | bytes accessed | tf_op | source)
XLA Modules:
  0.0 947.9 jit_solution(10972294971770210725)
XLA Ops:
  6.5 4.0 copy.64
  10.5 4.4 convert_bitcast_fusion
  14.9 9.6 %fusion.9 = f32[3,64,192,64]{2,3,1,0:T(8,128)} fusion(bf16[3,64,64,64]{3,2,1,0:T(8,128)(2,1)S(1)} %copy-done, bf16[3,192,64,64]{1,3,0,2:T(8,128)(2,1)S(1)} %convert_bitcast_fusion), kind=kOutput, calls=%fused_computation.24 | convolution fusion | flops 301989888 | bytes 15728640 | tf_op jit(solution)/shard_map/ptaj,pjak->ptjk/dot_general | solution.py:49
  24.5 11.7 %copy.68 = f32[3,192,4096]{2,1,0:T(8,128)} copy(f32[3,192,4096]{1,2,0:T(8,128)} %bitcast.132) | data formatting | bytes 18874368 | tf_op jit(solution)/shard_map/reshape | solution.py:58
  36.3 8.0 fusion.21
  44.3 5.9 copy.105
  54.2 121.8 %all-reduce.3.cloned.1.call-done = bf16[3,32,128,128]{3,2,1,0:T(8,128)(2,1)} async-done(((bf16[3,32,128,128]{3,2,1,0:T(8,128)(2,1)}), bf16[3,32,128,128]{3,2,1,0:T(8,128)(2,1)}) %all-reduce.3.cloned.1.call-update) | async-done | bytes 3145744 | tf_op jit(solution)/shard_map/psum | solution.py:15
  178.6 4.8 fusion.26
  187.3 7.1 gather_fusion
  194.4 14.5 %fusion.3 = bf16[2,32,16,1,64,128]{5,4,1,0,3,2:T(8,128)(2,1)} fusion(bf16[16,2,32,64,128]{4,3,2,1,0:T(8,128)(2,1)} %gather_fusion, pred[16]{0:T(512)(128)(4,1)S(1)} %compare_and_fusion, pred[16]{0:T(512)(128)(4,1)S(1)} %get-tuple-element.63), kind=kLoop, calls=%fused_computation.12 | loop fusion | flops 16777216 | bytes 33554464 | tf_op jit(solution)/shard_map/jit(_where)/select_n | solution.py:127
  208.9 6.9 all-to-all-start
  228.1 497.2 %collective-permute-done.1 = bf16[2,32,64,128]{3,2,1,0:T(8,128)(2,1)} collective-permute-done((bf16[2,32,64,128]{3,2,1,0:T(8,128)(2,1)}, bf16[2,32,64,128]{3,2,1,0:T(8,128)(2,1)}, u32[]{:S(2)}, u32[]{:S(2)}) %collective-permute-start.1) | collective-permute-done | bytes 1048608 | tf_op jit(solution)/shard_map/ppermute | solution.py:26
  727.9 4.1 fusion.56
  732.0 18.6 %all-gather = f32[512,128]{1,0:T(8,128)S(1)} all-gather(f32[32,128]{1,0:T(8,128)S(1)} %get-tuple-element.78), channel_id=2, replica_groups=mesh['dp'=16,'seq'=16] {'seq'}, dimensions={0}, use_global_device_ids=true | all-gather | bytes 278528 | tf_op jit(solution)/shard_map/all_gather | solution.py:32
  751.8 15.2 %all-gather.1 = f32[512,128]{1,0:T(8,128)S(1)} all-gather(f32[32,128]{1,0:T(8,128)S(1)} %fusion.18), channel_id=3, replica_groups=mesh['dp'=16,'seq'=16] {'seq'}, dimensions={0}, use_global_device_ids=true | all-gather | bytes 278528 | tf_op jit(solution)/shard_map/all_gather | solution.py:32
  769.5 11.1 %gather_fusion.1 = bf16[9,2,32,64,128]{4,3,2,1,0:T(8,128)(2,1)} fusion(bf16[2,32,16,64,128]{4,3,1,0,2:T(8,128)(2,1)} %bitcast.26, s32[1024]{0:T(1024)S(1)} %pad_clamp_fusion), kind=kCustom, calls=%fused_computation.1 | custom fusion | bytes 18874404 | tf_op jit(solution)/shard_map/jit(_take)/gather | solution.py:129
  780.6 9.6 %copy.86 = bf16[2,32,9,64,128]{4,3,2,1,0:T(8,128)(2,1)} copy(bf16[2,32,9,64,128]{4,3,1,0,2:T(8,128)(2,1)} %bitcast.141) | data formatting | bytes 18874368 | tf_op jit(solution)/shard_map/jit(_take)/gather | solution.py:129
  790.1 8.2 bitcast_select_fusion.1
  798.4 16.7 %pad_maximum_fusion = bf16[2,32,3,384,128]{4,3,2,1,0:T(8,128)(2,1)} fusion(bf16[2,32,3,192,128]{4,3,2,1,0:T(8,128)(2,1)} %bitcast_select_fusion.1, bf16[2,32,3,64,128]{4,3,2,1,0:T(8,128)(2,1)} %get-tuple-element.68, bf16[2,32,3,64,128]{4,3,2,1,0:T(8,128)(2,1)} %get-tuple-element.69, bf16[2,32,3,64,128]{4,3,2,1,0:T(8,128)(2,1)} %get-tuple-element.67), kind=kLoop, calls=%fused_computation.10 | loop fusion | flops 75497472 | bytes 37748736 | tf_op jit(solution)/shard_map/concatenate | solution.py:134
  815.0 11.6 %fusion.6 = (f32[32,3,64]{2,1,0:T(4,128)S(1)}, f32[32,3,64,384]{3,2,1,0:T(8,128)}) fusion(pred[3,384]{1,0:T(4,128)(4,1)S(1)} %concatenate.12, bf16[32,3,64,128]{3,2,1,0:T(8,128)(2,1)S(1)} %bitcast.144, bf16[2,32,3,384,128]{4,3,2,1,0:T(8,128)(2,1)} %pad_maximum_fusion), kind=kOutput, calls=%fused_computation.21 | convolution fusion | flops 611051520 | bytes 20472960 | tf_op jit(solution)/shard_map/hbqe,hbke->hbqk/dot_general | solution.py:152
  828.5 6.0 fusion.7
  836.8 6.5 divide_convert_fusion
  847.4 22.1 %slice.118 = f32[480,128,128]{2,1,0:T(8,128)} slice(f32[512,128,128]{2,1,0:T(8,128)} %all-gather.5.cloned.1.call-done), slice={[32:512], [0:128], [0:128]} | slice | bytes 62914560 | tf_op jit(solution)/shard_map/slice | solution.py:34
  869.5 67.9 %while.14 = (s32[]{:T(128)}, f32[32,128]{1,0:T(8,128)S(1)}, f32[32,128]{1,0:T(8,128)S(1)}, f32[32,128,128]{2,1,0:T(8,128)}, f32[15,32,128]{2,1,0:T(8,128)}, /*in...) while((s32[]{:T(128)}, f32[32,128]{1,0:T(8,128)S(1)}, f32[32,128]{1,0:T(8,128)S(1)}, ...), condition=%wide.region_4.5_spmd, body=%wide.region_3.4_spmd.sunk | while | flops 1597442 | bytes 6455397 | solution.py:35
  (126 shorter events, 108.8 us)
Async XLA Ops:
  6.5 8.4 copy-start
  6.5 169.5 %all-reduce.3.cloned.1.call-start = ((), (), s32[]{:S(2)}) async-start(), calls=%async_computation.1 | async-start | bytes 6291456 | tf_op jit(solution)/shard_map/psum | solution.py:15
  24.5 11.8 %copy-start.7 = (bf16[192,4096]{1,0:T(8,128)(2,1)S(1)}, bf16[192,4096]{1,0:T(8,128)(2,1)}, u32[]{:S(2)}) copy-start(bf16[192,4096]{1,0:T(8,128)(2,1)} %param.8) | copy-start | bytes 4718596
  24.5 11.8 %copy-start.11 = (bf16[3,16,4096]{2,1,0:T(8,128)(2,1)S(1)}, bf16[3,16,4096]{2,1,0:T(8,128)(2,1)}, u32[]{:S(2)}) copy-start(bf16[3,16,4096]{2,1,0:T(8,128)(2,1)} %param.12) | copy-start | bytes 1179652
  24.5 11.8 %copy-start.12 = (bf16[3,4096,16]{1,2,0:T(8,128)(2,1)S(1)}, bf16[3,4096,16]{1,2,0:T(8,128)(2,1)}, u32[]{:S(2)}) copy-start(bf16[3,4096,16]{1,2,0:T(8,128)(2,1)} %param.11) | copy-start | bytes 1179652
  54.0 790.3 %all-gather.5.cloned.1.call-start = ((), (), s32[]{:S(2)}) async-start(), calls=%async_computation.2 | async-start | bytes 35651584 | tf_op jit(solution)/shard_map/all_gather | solution.py:32
  178.6 4.8 copy-start.3
  183.4 2.1 copy-start.13
  208.9 560.5 %all-to-all-start = ((bf16[2,32,16,1,64,128]{5,4,1,0,3,2:T(8,128)(2,1)}), bf16[2,32,16,1,64,128]{5,4,1,0,3,2:T(8,128)(2,1)}, u32[]{:S(2)}, u32[]{:S(2)}) async-start(bf16[2,32,16,1,64,128]{5,4,1,0,3,2:T(8,128)(2,1)} %fusion.3), calls=%async_computation | async-start | bytes 33554432 | tf_op jit(solution)/shard_map/all_to_all | solution.py:128
  219.1 506.2 %collective-permute-start.1 = (bf16[2,32,64,128]{3,2,1,0:T(8,128)(2,1)}, bf16[2,32,64,128]{3,2,1,0:T(8,128)(2,1)}, u32[]{:S(2)}, u32[]{:S(2)}) collective-permute-start(bf16[2,32,64,128]{3,2,1,0:T(8,128)(2,1)} %get-tuple-element.71), channel_id=1, source_target_pairs={{1,0},{2,1},{3,2},{4,3},{5,4},{6,5},{7,6},{8,7},{9,8},{10,9},{11,1... | collective-permute-start | bytes 3145736 | tf_op jit(solution)/shard_map/ppermute | solution.py:26
  221.0 504.3 %collective-permute-start = (bf16[2,32,64,128]{3,2,1,0:T(8,128)(2,1)}, bf16[2,32,64,128]{3,2,1,0:T(8,128)(2,1)}, u32[]{:S(2)}, u32[]{:S(2)}) collective-permute-start(bf16[2,32,64,128]{3,2,1,0:T(8,128)(2,1)} %get-tuple-element.70), channel_id=1, source_target_pairs={{0,1},{1,2},{2,3},{3,4},{4,5},{5,6},{6,7},{7,8},{8,9},{9,10},{10,1... | collective-permute-start | bytes 3145736 | tf_op jit(solution)/shard_map/ppermute | solution.py:25
  727.9 23.4 %copy-start.4 = (f32[32,128,192]{1,2,0:T(8,128)S(1)}, f32[32,128,192]{1,2,0:T(8,128)}, u32[]{:S(2)}) copy-start(f32[32,128,192]{1,2,0:T(8,128)} %copy-done.3) | copy-start | bytes 9437188
  732.0 35.1 %copy-start.5 = (bf16[1,32,192,128]{3,2,1,0:T(8,128)(2,1)S(1)}, bf16[1,32,192,128]{3,2,1,0:T(8,128)(2,1)}, u32[]{:S(2)}) copy-start(bf16[1,32,192,128]{3,2,1,0:T(8,128)(2,1)} %slice.119) | copy-start | bytes 4718596
  767.0 13.5 %copy-start.10 = (f32[512,128]{1,0:T(8,128)}, f32[512,128]{1,0:T(8,128)S(1)}, u32[]{:S(2)}) copy-start(f32[512,128]{1,0:T(8,128)S(1)} %all-gather.1) | copy-start | bytes 786436
  798.4 16.7 %copy-start.6 = (bf16[1,32,192,128]{3,2,1,0:T(8,128)(2,1)S(1)}, bf16[1,32,192,128]{3,2,1,0:T(8,128)(2,1)}, u32[]{:S(2)}) copy-start(bf16[1,32,192,128]{3,2,1,0:T(8,128)(2,1)} %slice.119) | copy-start | bytes 4718596
  828.5 8.3 copy-start.2
  843.3 26.2 %copy-start.9 = (bf16[32,3,64,128]{3,2,1,0:T(8,128)(2,1)}, bf16[32,3,64,128]{3,2,1,0:T(8,128)(2,1)S(1)}, u32[]{:S(2)}) copy-start(bf16[32,3,64,128]{3,2,1,0:T(8,128)(2,1)S(1)} %divide_convert_fusion) | copy-start | bytes 4718596
  847.4 22.1 %slice-start = ((f32[512,128]{1,0:T(8,128)}), f32[480,128]{1,0:T(8,128)S(1)}, s32[]{:S(2)}) async-start(f32[512,128]{1,0:T(8,128)} %copy-done.10), calls=%async_computation.3 | async-start | bytes 491520 | tf_op jit(solution)/shard_map/slice | solution.py:34
  937.4 2.4 copy-start.8
  937.4 3.7 copy-start.1
Sparse Core Ops, SparseCore 0:
  54.1 121.8 all-reduce.2
  183.5 534.8 all-gather.4
where the time goes:
time: 950 us; the launch traced here: 948 us
  waiting for transfers between devices  619 us (65%)
  other arithmetic  126 us (13%)
  local copies, waits for them, and re-layouts  90.2 us (9%)
  matrix products  52.1 us (5%)
  blocking collectives  33.8 us (4%)
  between operations  13.7 us (1%)
  starting transfers between devices  12.7 us (1%)
    ppermute x1, waiting for transfers between devices, padded_2(): after = lax.ppermute(initial, axis, down)  497 us
    psum x1, waiting for transfers between devices, spread(): return lax.psum(jnp.where(mine, value, jnp.zeros_like(value)), axis)  122 us
    add x15, other arithmetic, combine(): numer_one * factor_one[:, :, None] + numer_two * factor_two[:, :, None]  56.9 us
    all_gather x2, blocking collectives, combined_all(): pieces = jax.tree.map(lambda part: lax.all_gather(part, axis), value)  33.8 us
    slice x4, local copies, waits for them, and re-layouts, combined_all(): tail = jax.tree.map(lambda part: part[1:], pieces)  22.8 us
    gather x2, local copies, waits for them, and re-layouts, per_device(): jnp.take(incoming.reshape(2, HEADS, seq_count * slot_count, BLK, head_siz...  20.7 us
  transfers between devices with their start and end apart: 5, of which 2 were waited for; matrix products, arithmetic and copies ran while one was open for 12% of the time, Pallas kernels for 0%

commit v1 on v0

--- a/solution.py
+++ b/solution.py
@@ -12,7 +12,7 @@
 
 def spread(value, axis, root):
     mine = lax.axis_index(axis) == root
-    return lax.psum(jnp.where(mine, value, jnp.zeros_like(value)), axis)
+    return jnp.sum(lax.all_gather(jnp.where(mine, value, jnp.zeros_like(value)), axis), axis=0)
 
 
 def padded_2(value, sides, width):

time: 950 us -> 1100 us (1.16)
  waiting for transfers between devices: 619 us -> 754 us
  other arithmetic: 126 us -> 140 us
    all_gather x0 -> x1, waiting for transfers between devices: none -> 258 us  [spread(): lax.all_gather(jnp.where(mine, value, jnp.zeros_like(value)), axis)]
    psum x1 -> x0, waiting for transfers between devices: 122 us -> none  [spread(): return lax.psum(jnp.where(mine, value, jnp.zeros_like(value)), axis)]
    reduce_sum x0 -> x1, other arithmetic: none -> 18.4 us  [spread(): jnp.sum(lax.all_gather(jnp.where(mine, value, jnp.zeros_like(value)), axi...]
  transfers between devices with their start and end apart: 5 -> 5, of which waited for: 2 -> 2; matrix products, arithmetic and copies ran while one was open for 12% -> 10% of each run, Pallas kernels for 0% -> 0%
where the time goes in v1:
time: 1100 us; the launch traced here: 1090 us
  waiting for transfers between devices  754 us (69%)
  other arithmetic  140 us (13%)
  local copies, waits for them, and re-layouts  91.3 us (8%)
  matrix products  50.5 us (5%)
  blocking collectives  34 us (3%)
  between operations  13.7 us (1%)
    ppermute x1, waiting for transfers between devices, padded_2(): after = lax.ppermute(initial, axis, down)  496 us
    all_gather x1, waiting for transfers between devices, spread(): lax.all_gather(jnp.where(mine, value, jnp.zeros_like(value)), axis)  258 us
    add x15, other arithmetic, combine(): numer_one * factor_one[:, :, None] + numer_two * factor_two[:, :, None]  56.9 us
    all_gather x2, blocking collectives, combined_all(): pieces = jax.tree.map(lambda part: lax.all_gather(part, axis), value)  34 us
    slice x4, local copies, waits for them, and re-layouts, combined_all(): tail = jax.tree.map(lambda part: part[1:], pieces)  22.9 us
  transfers between devices with their start and end apart: 5, of which 2 were waited for; matrix products, arithmetic and copies ran while one was open for 10% of the time, Pallas kernels for 0%

profile of v1, /device:TPU:1, one launch (start us, length us, event | category | flops | bytes accessed | tf_op | source)
XLA Modules:
  0.0 1094.3 jit_solution(4636813959671981526)
XLA Ops:
  6.5 4.0 copy.64
  10.5 4.4 convert_bitcast_fusion
  14.9 9.7 fusion.9
  24.6 11.7 %copy.68 = f32[3,192,4096]{2,1,0:T(8,128)} copy(f32[3,192,4096]{1,2,0:T(8,128)} %bitcast.133) | data formatting | bytes 18874368 | tf_op jit(solution)/shard_map/reshape | solution.py:58
  36.4 8.1 fusion.21
  44.4 5.8 copy.105
  54.2 257.5 %all-gather.7.cloned.1.call-done = bf16[48,32,128,128]{3,2,1,0:T(8,128)(2,1)} async-done(((bf16[3,32,128,128]{3,2,1,0:T(8,128)(2,1)}), bf16[48,32,128,128]{3,2,1,0:T(8,128)(2,1)}) %all-gather.7.cloned.1.call-update) | async-done | bytes 50331664 | tf_op jit(solution)/shard_map/all_gather | solution.py:15
  311.7 18.4 %reduce_sum.59 = bf16[3,32,128,128]{3,2,1,0:T(8,128)(2,1)} reduce(bf16[16,3,32,128,128]{4,3,2,1,0:T(8,128)(2,1)} %bitcast.141, bf16[]{:T(256)} %constant.55.clone.1), dimensions={0}, to_apply=%region_0.1 | reduce | flops 23592960 | bytes 53477376 | tf_op jit(solution)/shard_map/reduce_sum | solution.py:15
  332.6 4.7 fusion.26
  341.3 8.0 gather_fusion
  349.3 14.4 %fusion.3 = bf16[2,32,16,1,64,128]{5,4,1,0,3,2:T(8,128)(2,1)} fusion(bf16[16,2,32,64,128]{4,3,2,1,0:T(8,128)(2,1)} %gather_fusion, pred[16]{0:T(512)(128)(4,1)S(1)} %compare_and_fusion, pred[16]{0:T(512)(128)(4,1)S(1)} %get-tuple-element.63), kind=kLoop, calls=%fused_computation.12 | loop fusion | flops 16777216 | bytes 33554464 | tf_op jit(solution)/shard_map/jit(_where)/select_n | solution.py:127
  363.7 5.1 all-to-all-start
  380.9 496.0 %collective-permute-done.1 = bf16[2,32,64,128]{3,2,1,0:T(8,128)(2,1)} collective-permute-done((bf16[2,32,64,128]{3,2,1,0:T(8,128)(2,1)}, bf16[2,32,64,128]{3,2,1,0:T(8,128)(2,1)}, u32[]{:S(2)}, u32[]{:S(2)}) %collective-permute-start.1) | collective-permute-done | bytes 1048608 | tf_op jit(solution)/shard_map/ppermute | solution.py:26
  879.5 4.0 fusion.56
  883.5 10.8 gather_fusion.1
  894.3 9.6 copy.86
  904.0 8.3 bitcast_select_fusion.1
  912.3 15.4 %pad_maximum_fusion = bf16[2,32,3,384,128]{4,3,2,1,0:T(8,128)(2,1)} fusion(bf16[2,32,3,192,128]{4,3,2,1,0:T(8,128)(2,1)} %bitcast_select_fusion.1, bf16[2,32,3,64,128]{4,3,2,1,0:T(8,128)(2,1)} %get-tuple-element.68, bf16[2,32,3,64,128]{4,3,2,1,0:T(8,128)(2,1)} %get-tuple-element.69, bf16[2,32,3,64,128]{4,3,2,1,0:T(8,128)(2,1)S(1)} %get-tuple-element.67), kind=kLoop, calls=%fused_computation.10 | loop fusion | flops 75497472 | bytes 37748736 | tf_op jit(solution)/shard_map/concatenate | solution.py:134
  927.7 11.8 %fusion.6 = (f32[32,3,64]{2,1,0:T(4,128)S(1)}, f32[32,3,64,384]{3,2,1,0:T(8,128)}) fusion(pred[3,384]{1,0:T(4,128)(4,1)S(1)} %concatenate.12, bf16[32,3,64,128]{3,2,1,0:T(8,128)(2,1)S(1)} %bitcast.145, bf16[2,32,3,384,128]{4,3,2,1,0:T(8,128)(2,1)} %pad_maximum_fusion), kind=kOutput, calls=%fused_computation.21 | convolution fusion | flops 611051520 | bytes 20472960 | tf_op jit(solution)/shard_map/hbqe,hbke->hbqk/dot_general | solution.py:152
  939.5 18.6 %all-gather.1 = f32[512,128]{1,0:T(8,128)S(1)} all-gather(f32[32,128]{1,0:T(8,128)S(1)} %get-tuple-element.78), channel_id=3, replica_groups=mesh['dp'=16,'seq'=16] {'seq'}, dimensions={0}, use_global_device_ids=true | all-gather | bytes 278528 | tf_op jit(solution)/shard_map/all_gather | solution.py:32
  959.4 15.4 %all-gather.2 = f32[512,128]{1,0:T(8,128)S(1)} all-gather(f32[32,128]{1,0:T(8,128)S(1)} %fusion.18), channel_id=4, replica_groups=mesh['dp'=16,'seq'=16] {'seq'}, dimensions={0}, use_global_device_ids=true | all-gather | bytes 278528 | tf_op jit(solution)/shard_map/all_gather | solution.py:32
  983.1 6.5 divide_convert_fusion
  993.6 22.2 %slice.118 = f32[480,128,128]{2,1,0:T(8,128)} slice(f32[512,128,128]{2,1,0:T(8,128)} %all-gather.9.cloned.1.call-done), slice={[32:512], [0:128], [0:128]} | slice | bytes 62914560 | tf_op jit(solution)/shard_map/slice | solution.py:34
  1015.8 67.9 %while.14 = (s32[]{:T(128)}, f32[32,128]{1,0:T(8,128)S(1)}, f32[32,128]{1,0:T(8,128)S(1)}, f32[32,128,128]{2,1,0:T(8,128)}, f32[15,32,128]{2,1,0:T(8,128)}, /*in...) while((s32[]{:T(128)}, f32[32,128]{1,0:T(8,128)S(1)}, f32[32,128]{1,0:T(8,128)S(1)}, ...), condition=%wide.region_4.5_spmd, body=%wide.region_3.4_spmd.sunk | while | flops 1597442 | bytes 6455397 | solution.py:35
  (127 shorter events, 110.2 us)
Async XLA Ops:
  6.5 8.4 copy-start
  6.5 305.2 %all-gather.7.cloned.1.call-start = ((), (), s32[]{:S(2)}) async-start(), calls=%async_computation.1 | async-start | bytes 53477376 | tf_op jit(solution)/shard_map/all_gather | solution.py:15
  24.6 11.8 %copy-start.7 = (bf16[192,4096]{1,0:T(8,128)(2,1)S(1)}, bf16[192,4096]{1,0:T(8,128)(2,1)}, u32[]{:S(2)}) copy-start(bf16[192,4096]{1,0:T(8,128)(2,1)} %param.8) | copy-start | bytes 4718596
  24.6 11.8 %copy-start.11 = (bf16[3,16,4096]{2,1,0:T(8,128)(2,1)S(1)}, bf16[3,16,4096]{2,1,0:T(8,128)(2,1)}, u32[]{:S(2)}) copy-start(bf16[3,16,4096]{2,1,0:T(8,128)(2,1)} %param.12) | copy-start | bytes 1179652
  24.6 11.8 %copy-start.12 = (bf16[3,4096,16]{1,2,0:T(8,128)(2,1)S(1)}, bf16[3,4096,16]{1,2,0:T(8,128)(2,1)}, u32[]{:S(2)}) copy-start(bf16[3,4096,16]{1,2,0:T(8,128)(2,1)} %param.11) | copy-start | bytes 1179652
  54.0 936.5 %all-gather.9.cloned.1.call-start = ((), (), s32[]{:S(2)}) async-start(), calls=%async_computation.2 | async-start | bytes 35651584 | tf_op jit(solution)/shard_map/all_gather | solution.py:32
  332.6 4.8 copy-start.3
  337.4 2.1 copy-start.13
  363.7 519.8 %all-to-all-start = ((bf16[2,32,16,1,64,128]{5,4,1,0,3,2:T(8,128)(2,1)}), bf16[2,32,16,1,64,128]{5,4,1,0,3,2:T(8,128)(2,1)}, u32[]{:S(2)}, u32[]{:S(2)}) async-start(bf16[2,32,16,1,64,128]{5,4,1,0,3,2:T(8,128)(2,1)} %fusion.3), calls=%async_computation | async-start | bytes 33554432 | tf_op jit(solution)/shard_map/all_to_all | solution.py:128
  372.0 505.0 %collective-permute-start.1 = (bf16[2,32,64,128]{3,2,1,0:T(8,128)(2,1)}, bf16[2,32,64,128]{3,2,1,0:T(8,128)(2,1)}, u32[]{:S(2)}, u32[]{:S(2)}) collective-permute-start(bf16[2,32,64,128]{3,2,1,0:T(8,128)(2,1)} %get-tuple-element.71), channel_id=1, source_target_pairs={{1,0},{2,1},{3,2},{4,3},{5,4},{6,5},{7,6},{8,7},{9,8},{10,9},{11,1... | collective-permute-start | bytes 3145736 | tf_op jit(solution)/shard_map/ppermute | solution.py:26
  374.2 502.7 %collective-permute-start = (bf16[2,32,64,128]{3,2,1,0:T(8,128)(2,1)}, bf16[2,32,64,128]{3,2,1,0:T(8,128)(2,1)}, u32[]{:S(2)}, u32[]{:S(2)}) collective-permute-start(bf16[2,32,64,128]{3,2,1,0:T(8,128)(2,1)} %get-tuple-element.70), channel_id=1, source_target_pairs={{0,1},{1,2},{2,3},{3,4},{4,5},{5,6},{6,7},{7,8},{8,9},{9,10},{10,1... | collective-permute-start | bytes 3145736 | tf_op jit(solution)/shard_map/ppermute | solution.py:25
  912.2 15.4 %copy-start.5 = (bf16[1,32,192,128]{3,2,1,0:T(8,128)(2,1)S(1)}, bf16[1,32,192,128]{3,2,1,0:T(8,128)(2,1)}, u32[]{:S(2)}) copy-start(bf16[1,32,192,128]{3,2,1,0:T(8,128)(2,1)} %slice.119) | copy-start | bytes 4718596
  927.7 31.2 %copy-start.4 = (f32[32,128,192]{1,2,0:T(8,128)S(1)}, f32[32,128,192]{1,2,0:T(8,128)}, u32[]{:S(2)}) copy-start(f32[32,128,192]{1,2,0:T(8,128)} %copy-done.3) | copy-start | bytes 9437188
  939.5 35.3 %copy-start.6 = (bf16[3,32,128,128]{3,2,1,0:T(8,128)(2,1)S(1)}, bf16[3,32,128,128]{3,2,1,0:T(8,128)(2,1)}, u32[]{:S(2)}) copy-start(bf16[3,32,128,128]{3,2,1,0:T(8,128)(2,1)} %reduce_sum.59) | copy-start | bytes 9437188
  974.8 6.6 copy-start.10
  974.8 3.8 copy-start.2
  989.5 26.3 %copy-start.9 = (bf16[32,3,64,128]{3,2,1,0:T(8,128)(2,1)}, bf16[32,3,64,128]{3,2,1,0:T(8,128)(2,1)S(1)}, u32[]{:S(2)}) copy-start(bf16[32,3,64,128]{3,2,1,0:T(8,128)(2,1)S(1)} %divide_convert_fusion) | copy-start | bytes 4718596
  993.6 22.2 %slice-start = ((f32[512,128]{1,0:T(8,128)}), f32[480,128]{1,0:T(8,128)S(1)}, s32[]{:S(2)}) async-start(f32[512,128]{1,0:T(8,128)} %copy-done.10), calls=%async_computation.3 | async-start | bytes 491520 | tf_op jit(solution)/shard_map/slice | solution.py:34
  1083.8 2.4 copy-start.8
  1083.8 3.7 copy-start.1
Sparse Core Ops, SparseCore 0:
  54.1 257.5 all-gather.6
  337.5 532.4 all-gather.8
